TPU v7x, 32 devices: a whole 2x2x4 slice. The times are simulated.
32 devices in a mesh: view: 2 (over y), row: 2 (over x), col: 8 (over z, core).
Axes of the slice: x: 2, y: 2, z: 4, core: 2. Of those that a mesh axis runs over, the one named last changes fastest.
Arguments:
- inputs: bfloat16 [2, 512, 8192], P('view', 'col', 'row'), may hold values from -28 to 28, as said below
- weight: bfloat16 [8192, 8192], P('row', 'col'), may hold values from -0.0625 to 0.0625
Outputs:
- grad_hidden: bfloat16 [2, 512, 8192], P('view', 'col', 'row')
- grad_weight: float32 [8192, 8192], P('row', 'col')
Inputs may be any that keep to these rules, and one draw needn't show every extreme that they name: `inputs`: feature activations of the two views of a clip; each feature has its own scale.
All inputs are finite; a program needn't handle non-finite values.
Results may differ from a plain program's by a relative error of at most 0.025.
Values may be sent and summed in bfloat16 or wider, within the bound.
No kernel may reach another device: no remote copies, remote signals or barrier semaphores. Data moves between devices by JAX's collectives and lax.ppermute only.
A program may use at most 128 MiB of HBM per device.

v0:
```python
import math
import jax
import jax.numpy as jnp
from jax import lax
from jax.sharding import PartitionSpec as P

off_weight = 0.0051
norm_eps = 1e-05


def from_partner(block, axis, distance):
    count = lax.axis_size(axis)
    route = []
    for low in range(count):
        high = low | 1 << distance
        if high != low and high < count:
            route += [(low, high), (high, low)]
    return lax.ppermute(block, axis, route)


def shards(inputs, weight):
    hidden = lax.all_gather(inputs[0], "col", axis=0, tiled=True)
    batch = hidden.shape[0]
    columns = weight
    pre = lax.psum_scatter(
        lax.dot_general(
            columns, hidden, (((0,), (1,)), ((), ())), preferred_element_type=jnp.float32
        ).astype(jnp.bfloat16),
        "row",
        scatter_dimension=0,
        tiled=True,
    ).astype(jnp.float32)
    centred = pre - jnp.mean(pre, axis=1, keepdims=True)
    rstd = lax.rsqrt(jnp.mean(centred * centred, axis=1, keepdims=True) + norm_eps)
    own = (centred * rstd).astype(jnp.bfloat16)
    partner = from_partner(own, "view", 0)
    own_f = own.astype(jnp.float32)
    partner_f = partner.astype(jnp.float32)
    diag = jnp.sum(own_f * partner_f, axis=1, keepdims=True) / batch
    piece = lax.all_gather(partner, ("row", "col"), axis=0, tiled=True)
    corr = (
        lax.dot_general(own, piece, (((1,), (1,)), ((), ())), preferred_element_type=jnp.float32)
        / batch
    )
    mixed = jnp.dot(corr.astype(jnp.bfloat16), piece, preferred_element_type=jnp.float32)
    scale_diag = 2.0 * (diag - 1.0) - 2.0 * off_weight * diag
    dnorm = 2.0 * off_weight * mixed + scale_diag * partner_f
    inner = jnp.mean(dnorm * own_f, axis=1, keepdims=True)
    dpre = (rstd * (dnorm - jnp.mean(dnorm, axis=1, keepdims=True) - own_f * inner)).astype(
        jnp.bfloat16
    )
    grads = lax.all_gather(dpre, "row", axis=0, tiled=True)
    local_weight = lax.dot_general(
        hidden, grads, (((0,), (1,)), ((), ())), preferred_element_type=jnp.float32
    )
    grad_weight = lax.psum(local_weight.astype(jnp.bfloat16), "view").astype(
        jnp.float32
    ) / math.sqrt(2.0 * batch)
    columns = grads
    grad_hidden = lax.psum_scatter(
        lax.dot_general(
            columns, weight, (((0,), (1,)), ((), ())), preferred_element_type=jnp.float32
        ).astype(jnp.bfloat16),
        "col",
        scatter_dimension=0,
        tiled=True,
    )
    return (grad_hidden[None], grad_weight)


def solution(mesh):
    return jax.shard_map(
        shards,
        mesh=mesh,
        in_specs=(P("view", "col", "row"), P("row", "col")),
        out_specs=(P("view", "col", "row"), P("row", "col")),
        check_vma=False,
    )
```

profile of v0, /device:TPU:0, one launch (start us, length us, event | category | flops | bytes accessed | tf_op | source)
XLA Modules:
  0.0 486.3 jit_solution(11138176716313369393)
XLA Ops:
  7.2 0.0 all-gather.9.cloned.1.call-start
  7.2 0.7 all-gather.9.cloned.1.call-update
  7.9 0.0 reduce-scatter.3.cloned.1.call-start
  7.9 51.2 %all-gather.9.cloned.1.call-done = bf16[1,512,4096]{2,1,0:T(8,128)(2,1)} async-done(((bf16[1,64,4096]{2,1,0:T(8,128)(2,1)}), bf16[1,512,4096]{2,1,0:T(8,128)(2,1)}) %all-gather.9.cloned.1.call-update) | async-done | bytes 4194320 | tf_op jit(solution)/shard_map/all_gather | solution.py:22
  59.2 10.1 %fusion.4 = bf16[1024,512]{1,0:T(8,128)(2,1)} fusion(bf16[4096,1024]{1,0:T(8,128)(2,1)} %param.3, bf16[1,512,4096]{2,1,0:T(8,128)(2,1)} %all-gather.9.cloned.1.call-done), kind=kOutput, calls=%fused_computation.11 | convolution fusion | flops 4295491584 | bytes 13631488 | tf_op jit(solution)/shard_map/dot_general | solution.py:26
  69.3 0.0 reduce-scatter.3.cloned.1.call-update
  69.3 0.0 all-gather.5.cloned.1.call-start
  69.4 19.3 %reduce-scatter.3.cloned.1.call-done = bf16[512,512]{1,0:T(8,128)(2,1)} async-done(((bf16[1024,512]{1,0:T(8,128)(2,1)}), bf16[512,512]{1,0:T(8,128)(2,1)}) %reduce-scatter.3.cloned.1.call-update) | async-done | bytes 524304 | tf_op jit(solution)/shard_map/reduce_scatter | solution.py:25
  88.7 1.2 convert_reduce_fusion
  89.9 1.3 fusion.11
  91.2 1.3 fusion.12
  92.5 1.5 collective-permute-start
  94.0 12.0 %collective-permute-done = bf16[512,512]{1,0:T(8,128)(2,1)S(1)} collective-permute-done((bf16[512,512]{1,0:T(8,128)(2,1)S(1)}, bf16[512,512]{1,0:T(8,128)(2,1)S(1)}, u32[]{:S(2)}, u32[]{:S(2)}) %collective-permute-start) | collective-permute-done | bytes 524320 | tf_op jit(solution)/shard_map/ppermute | solution.py:18
  106.0 0.8 copy-done.1
  106.8 0.0 all-gather.5.cloned.1.call-update
  106.8 0.0 all-gather.7.cloned.1.call-start
  106.9 1.6 fusion.13
  108.6 72.7 %all-gather.5.cloned.1.call-done = bf16[8192,512]{1,0:T(8,128)(2,1)} async-done(((bf16[512,512]{1,0:T(8,128)(2,1)}), bf16[8192,512]{1,0:T(8,128)(2,1)}) %all-gather.5.cloned.1.call-update) | async-done | bytes 8388624 | tf_op jit(solution)/shard_map/all_gather | solution.py:40
  181.3 15.2 %fusion.19 = (f32[512]{0:T(512)S(1)}, f32[512]{0:T(512)S(1)}, f32[512,512]{1,0:T(8,128)S(1)}) fusion(bf16[512,512]{1,0:T(8,128)(2,1)S(1)} %fusion.12, bf16[512,512]{1,0:T(8,128)(2,1)} %copy-done.1, f32[512]{0:T(512)S(1)} %multiply_subtract_fusion, bf16[8192,512]{1,0:T(8,128)(2,1)} %all-gather.5.cloned.1.call-done), kind=kOutput, calls=%fused_computation.32 | convolution fusion | flops 8600420352 | bytes 10491904 | tf_op jit(solution)/shard_map/dot_general | solution.py:45
  196.6 1.1 fusion.17
  197.7 0.2 all-reduce.2.cloned.1.call-start
  197.9 19.8 %all-gather.7.cloned.1.call-done = bf16[1024,512]{1,0:T(8,128)(2,1)} async-done(((bf16[512,512]{1,0:T(8,128)(2,1)}), bf16[1024,512]{1,0:T(8,128)(2,1)}) %all-gather.7.cloned.1.call-update) | async-done | bytes 1048592 | tf_op jit(solution)/shard_map/all_gather | solution.py:52
  217.7 10.4 %convert_bitcast_fusion = bf16[4096,1024]{0,1:T(8,128)(2,1)} fusion(bf16[1024,512]{1,0:T(8,128)(2,1)} %all-gather.7.cloned.1.call-done, bf16[1,512,4096]{2,1,0:T(8,128)(2,1)} %all-gather.9.cloned.1.call-done), kind=kOutput, calls=%fused_computation.2 | convolution fusion | flops 4299161600 | bytes 13631488 | tf_op jit(solution)/shard_map/dot_general | solution.py:53
  228.2 0.0 all-reduce.2.cloned.1.call-update
  228.2 0.0 reduce-scatter.5.cloned.1.call-start
  228.2 1.1 copy-done.2
  229.4 9.6 %convolution_convert_fusion = bf16[512,4096]{1,0:T(8,128)(2,1)} fusion(bf16[1024,512]{1,0:T(8,128)(2,1)S(1)} %copy-done.2, bf16[4096,1024]{1,0:T(8,128)(2,1)} %param.3), kind=kOutput, calls=%fused_computation.3 | convolution fusion | flops 4297064448 | bytes 13631488 | tf_op jit(solution)/shard_map/dot_general | solution.py:61
  239.0 0.0 reduce-scatter.5.cloned.1.call-update
  239.0 187.4 %all-reduce.2.cloned.1.call-done = bf16[4096,1024]{0,1:T(8,128)(2,1)} async-done(((bf16[4096,1024]{0,1:T(8,128)(2,1)}), bf16[4096,1024]{0,1:T(8,128)(2,1)}) %all-reduce.2.cloned.1.call-update) | async-done | bytes 8388624 | tf_op jit(solution)/shard_map/psum | solution.py:56
  426.4 11.7 %convert_multiply_fusion = f32[4096,1024]{0,1:T(8,128)} fusion(bf16[4096,1024]{0,1:T(8,128)(2,1)} %all-reduce.2.cloned.1.call-done), kind=kLoop, calls=%fused_computation | loop fusion | flops 8388608 | bytes 25165824 | tf_op jit(solution)/shard_map/div | solution.py:56
  438.1 17.5 %copy.5 = f32[4096,1024]{1,0:T(8,128)} copy(f32[4096,1024]{0,1:T(8,128)} %convert_multiply_fusion) | data formatting | bytes 33554432
  455.6 23.8 %reduce-scatter.5.cloned.1.call-done = bf16[64,4096]{1,0:T(8,128)(2,1)} async-done(((bf16[512,4096]{1,0:T(8,128)(2,1)}), bf16[64,4096]{1,0:T(8,128)(2,1)}) %reduce-scatter.5.cloned.1.call-update) | async-done | bytes 524304 | tf_op jit(solution)/shard_map/reduce_scatter | solution.py:60
  (9 shorter events, 0.0 us)
Async XLA Ops:
  7.2 52.0 %all-gather.9.cloned.1.call-start = ((), (), s32[]{:S(2)}) async-start(), calls=%async_computation.7 | async-start | bytes 4718592 | tf_op jit(solution)/shard_map/all_gather | solution.py:22
  7.9 80.8 %reduce-scatter.3.cloned.1.call-start = ((), (), s32[]{:S(2)}) async-start(), calls=%async_computation.2 | async-start | bytes 1572864 | tf_op jit(solution)/shard_map/reduce_scatter | solution.py:25
  69.3 112.0 %all-gather.5.cloned.1.call-start = ((), (), s32[]{:S(2)}) async-start(), calls=%async_computation.3 | async-start | bytes 8912896 | tf_op jit(solution)/shard_map/all_gather | solution.py:40
  92.5 13.6 %collective-permute-start = (bf16[512,512]{1,0:T(8,128)(2,1)S(1)}, bf16[512,512]{1,0:T(8,128)(2,1)S(1)}, u32[]{:S(2)}, u32[]{:S(2)}) collective-permute-start(bf16[512,512]{1,0:T(8,128)(2,1)S(1)} %fusion.12), channel_id=1, source_target_pairs={{0,16},{16,0},{1,17},{17,1},{2,18},{18,2},{3,19},{19,3},{4,20},{20... | collective-permute-start | bytes 1572872 | tf_op jit(solution)/shard_map/ppermute | solution.py:18
  106.0 0.8 copy-start.1
  106.8 110.9 %all-gather.7.cloned.1.call-start = ((), (), s32[]{:S(2)}) async-start(), calls=%async_computation.4 | async-start | bytes 1572864 | tf_op jit(solution)/shard_map/all_gather | solution.py:52
  108.5 88.0 %copy-start = (bf16[512,512]{1,0:T(8,128)(2,1)S(1)}, bf16[512,512]{1,0:T(8,128)(2,1)}, u32[]{:S(2)}) copy-start(bf16[512,512]{1,0:T(8,128)(2,1)} %reduce-scatter.3.cloned.1.call-done) | copy-start | bytes 1572868
  197.7 228.7 %all-reduce.2.cloned.1.call-start = ((), (), s32[]{:S(2)}) async-start(), calls=%async_computation.6 | async-start | bytes 16777216 | tf_op jit(solution)/shard_map/psum | solution.py:56
  228.2 1.2 copy-start.2
  228.2 251.2 %reduce-scatter.5.cloned.1.call-start = ((), (), s32[]{:S(2)}) async-start(), calls=%async_computation.5 | async-start | bytes 4718592 | tf_op jit(solution)/shard_map/reduce_scatter | solution.py:60
Sparse Core Ops, SparseCore 0:
  9.6 49.5 all-gather.8
  69.4 19.1 reduce-scatter.2
  107.0 74.2 all-gather.4
  197.8 19.8 all-gather.6
  228.3 198.0 all-reduce.1
  429.1 50.2 reduce-scatter.4
where the time goes:
time: 487 us; the launch traced here: 486 us
  waiting for transfers between devices  387 us (79%)
  matrix products  45.4 us (9%)
  local copies, waits for them, and re-layouts  19.5 us (4%)
  other arithmetic  18.3 us (4%)
  between operations  14.2 us (3%)
    psum x1, waiting for transfers between devices, shards(): lax.psum(local_weight.astype(jnp.bfloat16), 'view').astype(jnp.float32)  187 us
    all_gather x1, waiting for transfers between devices, shards(): piece = lax.all_gather(partner, ('row', 'col'), axis=0, tiled=True)  72.7 us
    all_gather x1, waiting for transfers between devices, shards(): hidden = lax.all_gather(inputs[0], 'col', axis=0, tiled=True)  51.2 us
    reduce_scatter x1, waiting for transfers between devices, shards(): lax.psum_scatter(lax.dot_general(columns, weight, (((0,), (1,)), ((), ())...  23.8 us
    all_gather x1, waiting for transfers between devices, shards(): grads = lax.all_gather(dpre, 'row', axis=0, tiled=True)  19.8 us
    unnamed x7, local copies, waits for them, and re-layouts  19.5 us
    reduce_scatter x1, waiting for transfers between devices, shards(): lax.psum_scatter(lax.dot_general(columns, hidden, (((0,), (1,)), ((), ())...  19.3 us
    dot_general x1, matrix products, shards(): jnp.dot(corr.astype(jnp.bfloat16), piece, preferred_element_type=jnp.floa...  15.2 us
  transfers between devices with their start and end apart: 7, of which 7 were waited for; matrix products, arithmetic and copies ran while one was open for 8% of the time, Pallas kernels for 0%

commit v1 on v0

--- a/solution.py
+++ b/solution.py
@@ -19,7 +19,11 @@
 
 
 def shards(inputs, weight):
-    hidden = lax.all_gather(inputs[0], "col", axis=0, tiled=True)
+    local_x = inputs[0]
+    hidden = jnp.concatenate(
+        jax.lax.all_to_all(jnp.stack([local_x] * jax.lax.axis_size("col"), axis=0), "col", 0, 0),
+        axis=0,
+    )
     batch = hidden.shape[0]
     columns = weight
     pre = lax.psum_scatter(

time: 487 us -> 534 us (1.097)
  blocking collectives: 0 us -> 100 us
  waiting for transfers between devices: 387 us -> 335 us
    all_to_all x0 -> x1, blocking collectives: none -> 100 us  [shards(): jax.lax.all_to_all(jnp.stack([local_x] * jax.lax.axis_size('col'), axis=0...]
    all_gather x1 -> x0, waiting for transfers between devices: 51.2 us -> none  [shards(): hidden = lax.all_gather(inputs[0], 'col', axis=0, tiled=True)]
    unnamed x7 -> x11, local copies, waits for them, and re-layouts: 19.5 us -> 21.5 us
  transfers between devices with their start and end apart: 7 -> 6, of which waited for: 7 -> 6; matrix products, arithmetic and copies ran while one was open for 8% -> 8% of each run, Pallas kernels for 0% -> 0%
where the time goes in v1:
time: 534 us
  waiting for transfers between devices  335 us (63%)
  blocking collectives  100 us (19%)
  matrix products  40.8 us (8%)
  local copies, waits for them, and re-layouts  23.2 us (4%)
  other arithmetic  18.3 us (3%)
  between operations  13.9 us (3%)
    psum x1, waiting for transfers between devices, shards(): lax.psum(local_weight.astype(jnp.bfloat16), 'view').astype(jnp.float32)  187 us
    all_to_all x1, blocking collectives, shards(): jax.lax.all_to_all(jnp.stack([local_x] * jax.lax.axis_size('col'), axis=0...  100 us
    all_gather x1, waiting for transfers between devices, shards(): piece = lax.all_gather(partner, ('row', 'col'), axis=0, tiled=True)  72.7 us
    reduce_scatter x1, waiting for transfers between devices, shards(): lax.psum_scatter(lax.dot_general(columns, weight, (((0,), (1,)), ((), ())...  23.8 us
    unnamed x11, local copies, waits for them, and re-layouts  21.5 us
    all_gather x1, waiting for transfers between devices, shards(): grads = lax.all_gather(dpre, 'row', axis=0, tiled=True)  19.8 us
    reduce_scatter x1, waiting for transfers between devices, shards(): lax.psum_scatter(lax.dot_general(columns, hidden, (((0,), (1,)), ((), ())...  19.4 us
    dot_general x1, matrix products, shards(): jnp.dot(corr.astype(jnp.bfloat16), piece, preferred_element_type=jnp.floa...  15.2 us
  transfers between devices with their start and end apart: 6, of which 6 were waited for; matrix products, arithmetic and copies ran while one was open for 8% of the time, Pallas kernels for 0%

profile of v1, /device:TPU:0, one launch (start us, length us, event | category | flops | bytes accessed | tf_op | source)
XLA Modules:
  0.0 533.6 jit_solution(7468107121343447456)
XLA Ops:
  7.2 0.0 reduce-scatter.3.cloned.1.call-start
  7.2 1.7 stack.3
  8.9 100.4 %all_to_all.5 = bf16[8,64,4096]{2,1,0:T(8,128)(2,1)S(1)} all-to-all(bf16[8,64,4096]{2,1,0:T(8,128)(2,1)S(1)} %stack.3), channel_id=1, replica_groups=mesh['view'=2,'row'=2,'col'=8] {'col'}, dimensions={0} | all-to-all | bytes 8388608 | tf_op jit(solution)/shard_map/all_to_all | solution.py:24
  109.3 2.0 copy-done.1
  111.3 5.5 %convolution_convert_fusion.1 = bf16[1024,512]{1,0:T(8,128)(2,1)} fusion(bf16[4096,1024]{1,0:T(8,128)(2,1)S(1)} %copy-done.3, bf16[512,4096]{1,0:T(8,128)(2,1)S(1)} %bitcast.14), kind=kOutput, calls=%fused_computation.8 | convolution fusion | flops 4295491584 | bytes 13631488 | tf_op jit(solution)/shard_map/dot_general | solution.py:30
  116.8 0.0 reduce-scatter.3.cloned.1.call-update
  116.8 0.0 all-gather.3.cloned.1.call-start
  116.9 19.4 %reduce-scatter.3.cloned.1.call-done = bf16[512,512]{1,0:T(8,128)(2,1)} async-done(((bf16[1024,512]{1,0:T(8,128)(2,1)}), bf16[512,512]{1,0:T(8,128)(2,1)}) %reduce-scatter.3.cloned.1.call-update) | async-done | bytes 524304 | tf_op jit(solution)/shard_map/reduce_scatter | solution.py:29
  136.3 1.2 convert_reduce_fusion
  137.5 1.3 fusion.5
  138.9 1.3 fusion.6
  140.1 1.6 collective-permute-start
  141.7 12.0 %collective-permute-done = bf16[512,512]{1,0:T(8,128)(2,1)S(1)} collective-permute-done((bf16[512,512]{1,0:T(8,128)(2,1)S(1)}, bf16[512,512]{1,0:T(8,128)(2,1)S(1)}, u32[]{:S(2)}, u32[]{:S(2)}) %collective-permute-start) | collective-permute-done | bytes 524320 | tf_op jit(solution)/shard_map/ppermute | solution.py:18
  153.7 0.8 copy-done.2
  154.5 0.0 all-gather.3.cloned.1.call-update
  154.5 0.0 all-gather.5.cloned.1.call-start
  154.6 1.6 fusion.7
  156.2 72.7 %all-gather.3.cloned.1.call-done = bf16[8192,512]{1,0:T(8,128)(2,1)} async-done(((bf16[512,512]{1,0:T(8,128)(2,1)}), bf16[8192,512]{1,0:T(8,128)(2,1)}) %all-gather.3.cloned.1.call-update) | async-done | bytes 8388624 | tf_op jit(solution)/shard_map/all_gather | solution.py:44
  229.0 15.2 %fusion.13 = (f32[512]{0:T(512)S(1)}, f32[512]{0:T(512)S(1)}, f32[512,512]{1,0:T(8,128)S(1)}) fusion(bf16[512,512]{1,0:T(8,128)(2,1)S(1)} %fusion.6, bf16[512,512]{1,0:T(8,128)(2,1)} %copy-done.2, f32[512]{0:T(512)S(1)} %multiply_subtract_fusion, bf16[8192,512]{1,0:T(8,128)(2,1)} %all-gather.3.cloned.1.call-done), kind=kOutput, calls=%fused_computation.29 | convolution fusion | flops 8600420352 | bytes 10491904 | tf_op jit(solution)/shard_map/dot_general | solution.py:49
  244.2 1.1 fusion.11
  245.4 0.0 all-gather.5.cloned.1.call-update
  245.4 0.2 all-reduce.2.cloned.1.call-start
  245.6 19.8 %all-gather.5.cloned.1.call-done = bf16[1024,512]{1,0:T(8,128)(2,1)} async-done(((bf16[512,512]{1,0:T(8,128)(2,1)}), bf16[1024,512]{1,0:T(8,128)(2,1)}) %all-gather.5.cloned.1.call-update) | async-done | bytes 1048592 | tf_op jit(solution)/shard_map/all_gather | solution.py:56
  265.4 10.4 %convert_bitcast_fusion = bf16[4096,1024]{0,1:T(8,128)(2,1)} fusion(bf16[1024,512]{1,0:T(8,128)(2,1)} %all-gather.5.cloned.1.call-done, bf16[512,4096]{1,0:T(8,128)(2,1)} %bitcast.15), kind=kOutput, calls=%fused_computation.2 | convolution fusion | flops 4299161600 | bytes 13631488 | tf_op jit(solution)/shard_map/dot_general | solution.py:57
  275.9 0.0 all-reduce.2.cloned.1.call-update
  275.9 0.0 reduce-scatter.5.cloned.1.call-start
  275.9 1.1 copy-done.4
  277.1 9.6 %convolution_convert_fusion = bf16[512,4096]{1,0:T(8,128)(2,1)} fusion(bf16[1024,512]{1,0:T(8,128)(2,1)S(1)} %copy-done.4, bf16[4096,1024]{1,0:T(8,128)(2,1)} %param.3), kind=kOutput, calls=%fused_computation.3 | convolution fusion | flops 4297064448 | bytes 13631488 | tf_op jit(solution)/shard_map/dot_general | solution.py:65
  286.7 187.4 %all-reduce.2.cloned.1.call-done = bf16[4096,1024]{0,1:T(8,128)(2,1)} async-done(((bf16[4096,1024]{0,1:T(8,128)(2,1)}), bf16[4096,1024]{0,1:T(8,128)(2,1)}) %all-reduce.2.cloned.1.call-update) | async-done | bytes 8388624 | tf_op jit(solution)/shard_map/psum | solution.py:60
  474.1 11.7 %convert_multiply_fusion = f32[4096,1024]{0,1:T(8,128)} fusion(bf16[4096,1024]{0,1:T(8,128)(2,1)} %all-reduce.2.cloned.1.call-done), kind=kLoop, calls=%fused_computation | loop fusion | flops 8388608 | bytes 25165824 | tf_op jit(solution)/shard_map/div | solution.py:60
  485.8 17.5 %copy.5 = f32[4096,1024]{1,0:T(8,128)} copy(f32[4096,1024]{0,1:T(8,128)} %convert_multiply_fusion) | data formatting | bytes 33554432
  503.3 23.8 %reduce-scatter.5.cloned.1.call-done = bf16[64,4096]{1,0:T(8,128)(2,1)} async-done(((bf16[512,4096]{1,0:T(8,128)(2,1)}), bf16[64,4096]{1,0:T(8,128)(2,1)}) %reduce-scatter.5.cloned.1.call-update) | async-done | bytes 524304 | tf_op jit(solution)/shard_map/reduce_scatter | solution.py:64
  (12 shorter events, 0.1 us)
Async XLA Ops:
  7.2 129.2 %reduce-scatter.3.cloned.1.call-start = ((), (), s32[]{:S(2)}) async-start(), calls=%async_computation.3 | async-start | bytes 1572864 | tf_op jit(solution)/shard_map/reduce_scatter | solution.py:29
  7.2 104.1 %copy-start.3 = (bf16[4096,1024]{1,0:T(8,128)(2,1)S(1)}, bf16[4096,1024]{1,0:T(8,128)(2,1)}, u32[]{:S(2)}) copy-start(bf16[4096,1024]{1,0:T(8,128)(2,1)} %param.3) | copy-start | bytes 25165828
  109.3 2.0 copy-start.1
  116.8 112.1 %all-gather.3.cloned.1.call-start = ((), (), s32[]{:S(2)}) async-start(), calls=%async_computation.4 | async-start | bytes 8912896 | tf_op jit(solution)/shard_map/all_gather | solution.py:44
  140.1 13.6 %collective-permute-start = (bf16[512,512]{1,0:T(8,128)(2,1)S(1)}, bf16[512,512]{1,0:T(8,128)(2,1)S(1)}, u32[]{:S(2)}, u32[]{:S(2)}) collective-permute-start(bf16[512,512]{1,0:T(8,128)(2,1)S(1)} %fusion.6), channel_id=1, source_target_pairs={{0,16},{16,0},{1,17},{17,1},{2,18},{18,2},{3,19},{19,3},{4,20},{20... | collective-permute-start | bytes 1572872 | tf_op jit(solution)/shard_map/ppermute | solution.py:18
  153.7 0.8 copy-start.2
  154.5 110.9 %all-gather.5.cloned.1.call-start = ((), (), s32[]{:S(2)}) async-start(), calls=%async_computation.5 | async-start | bytes 1572864 | tf_op jit(solution)/shard_map/all_gather | solution.py:56
  156.2 88.0 %copy-start = (bf16[512,512]{1,0:T(8,128)(2,1)S(1)}, bf16[512,512]{1,0:T(8,128)(2,1)}, u32[]{:S(2)}) copy-start(bf16[512,512]{1,0:T(8,128)(2,1)} %reduce-scatter.3.cloned.1.call-done) | copy-start | bytes 1572868
  245.4 228.7 %all-reduce.2.cloned.1.call-start = ((), (), s32[]{:S(2)}) async-start(), calls=%async_computation.7 | async-start | bytes 16777216 | tf_op jit(solution)/shard_map/psum | solution.py:60
  275.9 1.2 copy-start.4
  275.9 251.2 %reduce-scatter.5.cloned.1.call-start = ((), (), s32[]{:S(2)}) async-start(), calls=%async_computation.6 | async-start | bytes 4718592 | tf_op jit(solution)/shard_map/reduce_scatter | solution.py:64
Sparse Core Ops, SparseCore 0:
  117.0 19.3 reduce-scatter.2
  154.6 74.2 all-gather.2
  245.5 19.8 all-gather.4
  276.0 198.0 all-reduce.1
  476.8 50.2 reduce-scatter.4
